TPU v7x, 512 devices: a whole 4x4x16 slice. The times are simulated.
512 devices in a mesh: dp: 64 (over y, z), mp: 8 (over x, core).
Axes of the slice: x: 4, y: 4, z: 16, core: 2. Of those that a mesh axis runs over, the one named last changes fastest.
Arguments:
- x_in: bfloat16 [25600, 2048], P('dp'), may hold values from -6 to 6
- cotangent: bfloat16 [25600, 7168], P('dp', 'mp'), may hold values from -6 to 6
- w_gate: bfloat16 [2048, 7168], P('dp', 'mp'), may hold values from -0.125 to 0.125
- w_up: bfloat16 [2048, 7168], P('dp', 'mp'), may hold values from -0.125 to 0.125
- send_counts: int32 [64, 64], P('dp'), may hold values from 0 to 4, as said below
- recv_counts: int32 [64, 64], P('dp'), may hold values from 0 to 4, as said below
Outputs:
- grad_x: bfloat16 [25600, 2048], P('dp', 'mp')
- grad_gate: float32 [2048, 7168], P('dp', 'mp')
Inputs may be any that keep to these rules, and one draw needn't show every extreme that they name: `send_counts`: each entry is 0 to 4. A quarter of the indices only send and the rest only receive; one sending index sends 4 rows to every receiver, so its live rows reach 400. recv_counts is the transpose of send_counts.
All inputs are finite; a program needn't handle non-finite values.
Results may differ from a plain program's by a relative error of at most 0.014.
Values may be sent and summed in bfloat16 or wider, within the bound.
A program may use at most 64 MiB of HBM per device.

v0:
```python
import jax
import jax.numpy as jnp
from jax import lax
from jax.sharding import PartitionSpec as P

BAL = 208


def contract_last(left, right):
    return lax.dot_general(
        left, right, (((1,), (1,)), ((), ())), preferred_element_type=jnp.float32
    )


def swiglu_back(x_rows, cot_rows, gate_full, up_full, live_mask):
    gate_val = jnp.dot(x_rows, gate_full, preferred_element_type=jnp.float32)
    up_val = jnp.dot(x_rows, up_full, preferred_element_type=jnp.float32)
    sig = jax.nn.sigmoid(gate_val)
    cot_val = cot_rows.astype(jnp.float32)
    d_gate = jnp.where(
        live_mask[:, None], cot_val * up_val * sig * (1.0 + gate_val * (1.0 - sig)), 0.0
    ).astype(jnp.bfloat16)
    d_up = jnp.where(live_mask[:, None], cot_val * gate_val * sig, 0.0).astype(jnp.bfloat16)
    partial_value = contract_last(d_gate, gate_full) + contract_last(d_up, up_full)
    return (partial_value, d_gate)


def group_sum(partial_value):
    return lax.psum_scatter(
        partial_value.astype(jnp.bfloat16), "mp", scatter_dimension=1, tiled=True
    )


def on_device(x_in, cotangent, w_gate, w_up, send_counts, recv_counts):
    rows_cap = x_in.shape[0]
    width = x_in.shape[1]
    dev_count = lax.axis_size("dp")
    gate_full, up_full = (
        lax.all_gather(w_gate, "dp", axis=0, tiled=True),
        lax.all_gather(w_up, "dp", axis=0, tiled=True),
    )
    sent = send_counts[0]
    got = recv_counts[0]
    live_rows = BAL + jnp.sum(sent) - jnp.sum(got)
    live_mask = jnp.arange(rows_cap) < live_rows
    partial_value, d_gate = swiglu_back(x_in, cotangent, gate_full, up_full, live_mask)
    grad_x = group_sum(partial_value)
    block_rows = width // dev_count
    whole = lax.dot_general(
        x_in, d_gate, (((0,), (0,)), ((), ())), preferred_element_type=jnp.float32
    )
    pieces = lax.all_to_all(
        whole.reshape(dev_count, block_rows, whole.shape[1]),
        "dp",
        split_axis=0,
        concat_axis=0,
        tiled=True,
    )
    grad_gate = jnp.sum(pieces, axis=0)
    return (grad_x, grad_gate)


def solution(mesh):
    return jax.shard_map(
        on_device,
        mesh=mesh,
        in_specs=(
            P("dp", None),
            P("dp", "mp"),
            P("dp", "mp"),
            P("dp", "mp"),
            P("dp", None),
            P("dp", None),
        ),
        out_specs=(P("dp", "mp"), P("dp", "mp")),
        check_vma=False,
    )
```

profile of v0, /device:TPU:40, one launch (start us, length us, event | category | flops | bytes accessed | tf_op | source)
XLA Modules:
  0.0 655.1 jit_solution(2757115259836697737)
XLA Ops:
  7.2 0.0 copy-start
  7.2 0.0 all-gather.5.cloned.1.call-start
  7.2 0.7 all-gather.5.cloned.1.call-update
  7.9 0.0 all-gather.3.cloned.1.call-start
  8.0 0.7 all-gather.3.cloned.1.call-update
  8.7 1.3 reduce_sum.28
  10.0 1.3 reduce_sum.27
  12.6 0.0 copy-start.2
  12.6 146.4 %all-gather.5.cloned.1.call-done = bf16[2048,896]{1,0:T(8,128)(2,1)} async-done(((bf16[32,896]{1,0:T(8,128)(2,1)}), bf16[2048,896]{1,0:T(8,128)(2,1)}) %all-gather.5.cloned.1.call-update) | async-done | bytes 3670032 | tf_op jit(solution)/shard_map/all_gather | solution.py:39
  159.0 0.0 copy-done
  159.0 5.0 fusion.11
  164.0 137.7 %all-gather.3.cloned.1.call-done = bf16[2048,896]{1,0:T(8,128)(2,1)} async-done(((bf16[32,896]{1,0:T(8,128)(2,1)}), bf16[2048,896]{1,0:T(8,128)(2,1)}) %all-gather.3.cloned.1.call-update) | async-done | bytes 3670032 | tf_op jit(solution)/shard_map/all_gather | solution.py:40
  301.7 0.0 copy-done.2
  301.7 4.6 select_convert_fusion
  306.2 5.1 convolution_bitcast_fusion
  311.4 8.6 %copy.8 = f32[2048,896]{1,0:T(8,128)} copy(f32[2048,896]{0,1:T(8,128)} %convolution_bitcast_fusion) | data formatting | bytes 14680064 | tf_op jit(solution)/shard_map/dot_general | solution.py:49
  320.0 10.2 %all-to-all-start = ((f32[64,32,896]{2,1,0:T(8,128)}), f32[64,32,896]{2,1,0:T(8,128)}, u32[]{:S(2)}, u32[]{:S(2)}) async-start(f32[64,32,896]{2,1,0:T(8,128)} %bitcast.12), calls=%async_computation.1 | async-start | bytes 14680064 | tf_op jit(solution)/shard_map/all_to_all | solution.py:52
  330.2 0.0 reduce-scatter.2.cloned.1.call-start
  330.2 0.0 copy-start.1
  330.3 4.1 fusion.12
  334.4 3.1 add_convert_fusion
  337.5 0.0 reduce-scatter.2.cloned.1.call-update
  337.5 307.0 %all-to-all-done = f32[64,32,896]{2,1,0:T(8,128)} async-done(((f32[64,32,896]{2,1,0:T(8,128)}), f32[64,32,896]{2,1,0:T(8,128)}, u32[]{:S(2)}, u32[]{:S(2)}) %all-to-all-start) | async-done | bytes 7340064 | tf_op jit(solution)/shard_map/all_to_all | solution.py:52
  644.5 4.1 reduce_sum.29
  (5 shorter events, 0.0 us)
Async XLA Ops:
  7.2 151.8 %copy-start = (bf16[400,2048]{1,0:T(8,128)(2,1)S(1)}, bf16[400,2048]{1,0:T(8,128)(2,1)}, u32[]{:S(2)}) copy-start(bf16[400,2048]{1,0:T(8,128)(2,1)} %param.6) | copy-start | bytes 4915204
  7.2 151.8 %all-gather.5.cloned.1.call-start = ((), (), s32[]{:S(2)}) async-start(), calls=%async_computation.3 | async-start | bytes 3727360 | tf_op jit(solution)/shard_map/all_gather | solution.py:39
  7.9 293.8 %all-gather.3.cloned.1.call-start = ((), (), s32[]{:S(2)}) async-start(), calls=%async_computation.2 | async-start | bytes 3727360 | tf_op jit(solution)/shard_map/all_gather | solution.py:40
  12.6 289.1 %copy-start.2 = (bf16[400,896]{1,0:T(8,128)(2,1)S(1)}, bf16[400,896]{1,0:T(8,128)(2,1)}, u32[]{:S(2)}) copy-start(bf16[400,896]{1,0:T(8,128)(2,1)} %param.7) | copy-start | bytes 2150404
  320.0 324.5 %all-to-all-start = ((f32[64,32,896]{2,1,0:T(8,128)}), f32[64,32,896]{2,1,0:T(8,128)}, u32[]{:S(2)}, u32[]{:S(2)}) async-start(f32[64,32,896]{2,1,0:T(8,128)} %bitcast.12), calls=%async_computation.1 | async-start | bytes 14680064 | tf_op jit(solution)/shard_map/all_to_all | solution.py:52
  330.2 318.4 %reduce-scatter.2.cloned.1.call-start = ((), (), s32[]{:S(2)}) async-start(), calls=%async_computation.4 | async-start | bytes 1843200 | tf_op jit(solution)/shard_map/reduce_scatter | solution.py:29
  330.2 4.1 copy-start.1
  330.2 4.1 copy-start.3
Sparse Core Ops, SparseCore 0:
  11.0 147.9 all-gather.4
  161.9 139.7 all-gather.2
  337.6 42.0 reduce-scatter.1
where the time goes:
time: 656 us; the launch traced here: 655 us
  waiting for transfers between devices  592 us (90%)
  matrix products  21.9 us (3%)
  between operations  15.1 us (2%)
  starting transfers between devices  10.3 us (2%)
  local copies, waits for them, and re-layouts  8.61 us (1%)
  other arithmetic  6.68 us (1%)
    all_to_all x1, waiting for transfers between devices, on_device(): lax.all_to_all(whole.reshape(dev_count, block_rows, whole.shape[1]), 'dp'...  307 us
    all_gather x1, waiting for transfers between devices, on_device(): lax.all_gather(w_gate, 'dp', axis=0, tiled=True)  146 us
    all_gather x1, waiting for transfers between devices, on_device(): lax.all_gather(w_up, 'dp', axis=0, tiled=True)  138 us
  transfers between devices with their start and end apart: 4, of which 3 were waited for; matrix products, arithmetic and copies ran while one was open for 3% of the time, Pallas kernels for 0%

commit v1 on v0

--- a/solution.py
+++ b/solution.py
@@ -37,7 +37,9 @@
     dev_count = lax.axis_size("dp")
     gate_full, up_full = (
         lax.all_gather(w_gate, "dp", axis=0, tiled=True),
-        lax.all_gather(w_up, "dp", axis=0, tiled=True),
+        jnp.concatenate(
+            lax.all_to_all(jnp.stack([w_up] * lax.axis_size("dp")), "dp", 0, 0), axis=0
+        ),
     )
     sent = send_counts[0]
     got = recv_counts[0]

time: 656 us -> 595 us (0.907)
  the two profiles are of different devices: /device:TPU:40 before, /device:TPU:6 now
where the time goes in v1:
time: 595 us; the launch traced here: 594 us
  waiting for transfers between devices  508 us (85%)
  starting transfers between devices  29.6 us (5%)
  matrix products  24 us (4%)
  between operations  15.4 us (3%)
  local copies, waits for them, and re-layouts  11.6 us (2%)
    all_to_all x1, waiting for transfers between devices, on_device(): lax.all_to_all(whole.reshape(dev_count, block_rows, whole.shape[1]), 'dp'...  310 us
    all_gather x1, waiting for transfers between devices, on_device(): lax.all_gather(w_gate, 'dp', axis=0, tiled=True)  198 us
    all_to_all x1, starting transfers between devices, on_device(): lax.all_to_all(jnp.stack([w_up] * lax.axis_size('dp')), 'dp', 0, 0)  19.1 us
  transfers between devices with their start and end apart: 4, of which 2 were waited for; matrix products, arithmetic and copies ran while one was open for 3% of the time, Pallas kernels for 0%

profile of v1, /device:TPU:6, one launch (start us, length us, event | category | flops | bytes accessed | tf_op | source)
XLA Modules:
  0.0 594.1 jit_solution(46315861394344706)
XLA Ops:
  7.2 0.0 copy-start
  7.2 3.0 stack.2
  10.2 19.1 %all-to-all-start = ((bf16[64,32,896]{2,1,0:T(8,128)(2,1)}), bf16[64,32,896]{2,1,0:T(8,128)(2,1)}, u32[]{:S(2)}, u32[]{:S(2)}) async-start(bf16[64,32,896]{2,1,0:T(8,128)(2,1)} %stack.2), calls=%async_computation | async-start | bytes 7340032 | tf_op jit(solution)/shard_map/all_to_all | solution.py:41
  29.3 0.0 all-gather.2.cloned.1.call-start
  29.3 0.7 all-gather.2.cloned.1.call-update
  30.0 0.0 copy-done.2
  30.0 0.6 reduce_sum.28
  30.7 0.0 copy-done.3
  30.7 0.6 reduce_sum.27
  32.6 0.0 copy-start.1
  32.6 197.9 %all-gather.2.cloned.1.call-done = bf16[2048,896]{1,0:T(8,128)(2,1)} async-done(((bf16[32,896]{1,0:T(8,128)(2,1)}), bf16[2048,896]{1,0:T(8,128)(2,1)}) %all-gather.2.cloned.1.call-update) | async-done | bytes 3670032 | tf_op jit(solution)/shard_map/all_gather | solution.py:39
  230.5 0.0 copy-done
  230.5 5.0 fusion.11
  235.5 0.0 all-to-all-done
  235.5 4.6 select_convert_fusion
  240.1 5.1 convolution_bitcast_fusion
  245.2 8.6 %copy.8 = f32[2048,896]{1,0:T(8,128)} copy(f32[2048,896]{0,1:T(8,128)} %convolution_bitcast_fusion) | data formatting | bytes 14680064 | tf_op jit(solution)/shard_map/dot_general | solution.py:51
  253.8 10.4 %all-to-all-start.1 = ((f32[64,32,896]{2,1,0:T(8,128)}), f32[64,32,896]{2,1,0:T(8,128)}, u32[]{:S(2)}, u32[]{:S(2)}) async-start(f32[64,32,896]{2,1,0:T(8,128)} %bitcast.13), calls=%async_computation.2 | async-start | bytes 14680064 | tf_op jit(solution)/shard_map/all_to_all | solution.py:54
  264.2 0.0 reduce-scatter.2.cloned.1.call-start
  264.3 4.0 fusion.12
  268.3 5.2 add_convert_fusion
  273.5 0.0 reduce-scatter.2.cloned.1.call-update
  273.6 309.6 %all-to-all-done.1 = f32[64,32,896]{2,1,0:T(8,128)} async-done(((f32[64,32,896]{2,1,0:T(8,128)}), f32[64,32,896]{2,1,0:T(8,128)}, u32[]{:S(2)}, u32[]{:S(2)}) %all-to-all-start.1) | async-done | bytes 7340064 | tf_op jit(solution)/shard_map/all_to_all | solution.py:54
  583.1 4.1 reduce_sum.29
  (7 shorter events, 0.0 us)
Async XLA Ops:
  7.2 223.3 %copy-start = (bf16[400,2048]{1,0:T(8,128)(2,1)S(1)}, bf16[400,2048]{1,0:T(8,128)(2,1)}, u32[]{:S(2)}) copy-start(bf16[400,2048]{1,0:T(8,128)(2,1)} %param.6) | copy-start | bytes 4915204
  10.2 19.8 %copy-start.2 = (s32[1,64]{1,0:T(1,128)S(1)}, s32[1,64]{1,0:T(1,128)}, u32[]{:S(2)}) copy-start(s32[1,64]{1,0:T(1,128)} %param.11) | copy-start | bytes 772
  10.2 20.5 %copy-start.3 = (s32[1,64]{1,0:T(1,128)S(1)}, s32[1,64]{1,0:T(1,128)}, u32[]{:S(2)}) copy-start(s32[1,64]{1,0:T(1,128)} %param.10) | copy-start | bytes 772
  10.2 225.3 %all-to-all-start = ((bf16[64,32,896]{2,1,0:T(8,128)(2,1)}), bf16[64,32,896]{2,1,0:T(8,128)(2,1)}, u32[]{:S(2)}, u32[]{:S(2)}) async-start(bf16[64,32,896]{2,1,0:T(8,128)(2,1)} %stack.2), calls=%async_computation | async-start | bytes 7340032 | tf_op jit(solution)/shard_map/all_to_all | solution.py:41
  29.3 201.2 %all-gather.2.cloned.1.call-start = ((), (), s32[]{:S(2)}) async-start(), calls=%async_computation.3 | async-start | bytes 3727360 | tf_op jit(solution)/shard_map/all_gather | solution.py:39
  32.6 202.9 %copy-start.1 = (bf16[400,896]{1,0:T(8,128)(2,1)S(1)}, bf16[400,896]{1,0:T(8,128)(2,1)}, u32[]{:S(2)}) copy-start(bf16[400,896]{1,0:T(8,128)(2,1)} %param.7) | copy-start | bytes 2150404
  253.8 329.3 %all-to-all-start.1 = ((f32[64,32,896]{2,1,0:T(8,128)}), f32[64,32,896]{2,1,0:T(8,128)}, u32[]{:S(2)}, u32[]{:S(2)}) async-start(f32[64,32,896]{2,1,0:T(8,128)} %bitcast.13), calls=%async_computation.2 | async-start | bytes 14680064 | tf_op jit(solution)/shard_map/all_to_all | solution.py:54
  264.2 323.0 %reduce-scatter.2.cloned.1.call-start = ((), (), s32[]{:S(2)}) async-start(), calls=%async_computation.4 | async-start | bytes 1843200 | tf_op jit(solution)/shard_map/reduce_scatter | solution.py:29
  264.3 4.0 copy-start.4
Sparse Core Ops, SparseCore 0:
  33.1 197.3 all-gather.1
  273.7 38.5 reduce-scatter.1
